TPU v7x, 512 devices: a whole 4x4x16 slice. The times are simulated.
512 devices in a mesh: aa: 16 (over z_hi, x), ba: 32 (over z_lo, y, core).
Axes of the slice: x: 4, y: 4, z: 16 (z_hi: 4, z_lo: 4; z = z_hi * 4 + z_lo), core: 2. Of those that a mesh axis runs over, the one named last changes fastest.
Arguments:
- amplitudes: float32 [256, 256, 1024], P('aa', 'ba'), may hold values from -4 to 4
- driving: bfloat16 [256, 256, 1024], P('aa', 'ba'), may hold values from -6 to 6
- ladder: bfloat16 [1024, 1024], P('aa', 'ba'), may hold values from -0.09375 to 0.09375
- block_mask: int32 [16, 16], replicated, may hold values 0 or 1
- virt_energy: float32 [256], replicated, may hold values from 0.5 to 3
- occ_energy: float32 [32], replicated, may hold values from -3 to -0.5
Outputs:
- updated: float32 [256, 256, 1024], P('aa', 'ba')
All inputs are finite; a program needn't handle non-finite values.
Results may differ from a plain program's by a relative error of at most 0.0003.
Values may be sent and summed in bfloat16 or wider, within the bound.
A program may use at most 64 MiB of HBM per device.

v0:
```python
import jax
import jax.numpy as jnp
from jax import lax
from jax.sharding import PartitionSpec as P

O = 32
BLOCK = 64
ITERS = 2


def mirror_tile(moved):
    first_rows = moved.shape[0]
    second_rows = moved.shape[1]
    return (
        moved.reshape(first_rows, second_rows, O, O)
        .transpose(1, 0, 3, 2)
        .reshape(second_rows, first_rows, O * O)
    )


def mirrored(ladder_term):
    moved = lax.all_to_all(
        ladder_term.astype(jnp.bfloat16), "ba", split_axis=2, concat_axis=1, tiled=True
    ).astype(ladder_term.dtype)
    moved = lax.all_to_all(
        moved.astype(jnp.bfloat16), "aa", split_axis=1, concat_axis=0, tiled=True
    ).astype(moved.dtype)
    moved = lax.all_to_all(
        moved.astype(jnp.bfloat16), "ba", split_axis=0, concat_axis=2, tiled=True
    ).astype(moved.dtype)
    return mirror_tile(moved)


def product(field, matrix):
    rows_a = field.shape[0]
    cols_b = field.shape[1]
    pairs = field.shape[2]
    return jnp.dot(
        field.reshape(rows_a * cols_b, pairs),
        matrix,
        precision=lax.Precision.HIGHEST,
        preferred_element_type=jnp.float32,
    ).reshape(rows_a, cols_b, pairs)


def on_device(amplitudes, driving, ladder, block_mask, virt_energy, occ_energy):
    rows_a = amplitudes.shape[0]
    cols_b = amplitudes.shape[1]
    pairs = amplitudes.shape[2]
    partial_rows = lax.all_gather(ladder, "ba", axis=1, tiled=True)
    whole = lax.all_gather(partial_rows, "aa", axis=0, tiled=True)
    blocks = pairs // BLOCK
    kept = block_mask.astype(jnp.float32)[:, None, :, None]
    weights = (whole.astype(jnp.float32).reshape(blocks, BLOCK, blocks, BLOCK) * kept).reshape(
        pairs, pairs
    )
    energy_a = lax.dynamic_slice_in_dim(virt_energy, lax.axis_index("aa") * rows_a, rows_a)
    energy_b = lax.dynamic_slice_in_dim(virt_energy, lax.axis_index("ba") * cols_b, cols_b)
    pair_energy = (occ_energy[:, None] + occ_energy[None, :]).reshape(pairs)
    denominator = energy_a[:, None, None] + energy_b[None, :, None] - pair_energy[None, None, :]
    driving_wide = driving.astype(jnp.float32)
    for iteration in range(ITERS):
        ladder_term = product(amplitudes, weights)
        partner = mirrored(ladder_term)
        amplitudes = (driving_wide + ladder_term + partner) / denominator
    return amplitudes


def solution(mesh):
    placed = (P("aa", "ba", None), P("aa", "ba", None), P("aa", "ba"), P(), P(), P())
    return jax.shard_map(
        on_device, mesh=mesh, in_specs=placed, out_specs=P("aa", "ba", None), check_vma=False
    )
```

profile of v0, /device:TPU:1, one launch (start us, length us, event | category | flops | bytes accessed | tf_op | source)
XLA Modules:
  0.0 328.5 jit_solution(6033978209433725267)
XLA Ops:
  6.5 47.0 %all_gather.6 = bf16[64,1024]{0,1:T(8,128)(2,1)S(1)} all-gather(bf16[64,32]{0,1:T(8,128)(2,1)} %param.8), channel_id=1, replica_groups=mesh['aa'=16,'ba'=32] {'ba'}, dimensions={1}, use_global_device_ids=true | all-gather | bytes 135168 | tf_op jit(solution)/shard_map/all_gather | solution.py:50
  55.1 3.8 %mul.17 = f32[16,64,16,64]{3,2,1,0:T(8,128)} broadcast(f32[16,16]{1,0:T(8,128)S(1)} %convert_element_type.43), dimensions={0,2} | broadcast | bytes 4195328 | tf_op jit(solution)/shard_map/mul | solution.py:54
  58.9 7.6 %mul.18 = f32[1024,1024]{1,0:T(8,128)} reshape(f32[16,64,16,64]{3,2,1,0:T(8,128)} %mul.17) | data formatting | bytes 8388608 | tf_op jit(solution)/shard_map/mul | solution.py:54
  66.5 80.3 %all-gather.2.cloned.1.call-done = bf16[1024,1024]{1,0:T(8,128)(2,1)} async-done(((bf16[64,1024]{1,0:T(8,128)(2,1)}), bf16[1024,1024]{1,0:T(8,128)(2,1)}) %all-gather.2.cloned.1.call-update) | async-done | bytes 2097168 | tf_op jit(solution)/shard_map/all_gather | solution.py:51
  146.8 6.3 %fusion.9 = (bf16[16,8,1024]{2,1,0:T(8,128)(2,1)S(1)}, f32[16,8,1024]{2,1,0:T(8,128)}) fusion(f32[16,8,1024]{2,1,0:T(8,128)S(1)} %copy-done, f32[1024,1024]{1,0:T(8,128)} %mul.18, bf16[1024,1024]{1,0:T(8,128)(2,1)} %all-gather.2.cloned.1.call-done), kind=kOutput, calls=%fused_computation.18 | convolution fusion | flops 1612840960 | bytes 7602176 | tf_op jit(solution)/shard_map/dot_general | solution.py:38
  153.1 1.6 copy.29
  154.8 2.2 reshape.97
  157.0 17.5 %all_to_all.90 = bf16[32,2,2048]{2,1,0:T(2,128)(2,1)S(1)} all-to-all(bf16[32,2,2048]{2,1,0:T(2,128)(2,1)S(1)} %reshape.97), channel_id=1, replica_groups=mesh['aa'=16,'ba'=32] {'ba'}, dimensions={0} | all-to-all | bytes 524288 | tf_op jit(solution)/shard_map/all_to_all | solution.py:22
  174.6 1.4 reshape.98
  176.0 3.1 copy.30
  179.1 1.9 copy.42
  182.0 23.4 %all_to_all.91 = bf16[16,2,4096]{2,1,0:T(2,128)(2,1)S(1)} all-to-all(bf16[16,2,4096]{2,1,0:T(2,128)(2,1)S(1)} %reshape.99), channel_id=1, replica_groups=mesh['aa'=16,'ba'=32] {'aa'}, dimensions={0} | all-to-all | bytes 524288 | tf_op jit(solution)/shard_map/all_to_all | solution.py:25
  206.3 1.7 reshape.101
  208.0 8.6 %all-to-all-start.2 = ((bf16[32,2,2048]{2,1,0:T(2,128)(2,1)}), bf16[32,2,2048]{2,1,0:T(2,128)(2,1)S(1)}, u32[]{:S(2)}, u32[]{:S(2)}) async-start(bf16[32,2,2048]{2,1,0:T(2,128)(2,1)} %reshape.101), calls=%async_computation.2 | async-start | bytes 524288 | tf_op jit(solution)/shard_map/all_to_all | solution.py:28
  217.0 10.7 %all-to-all-done.2 = bf16[32,2,2048]{2,1,0:T(2,128)(2,1)S(1)} async-done(((bf16[32,2,2048]{2,1,0:T(2,128)(2,1)}), bf16[32,2,2048]{2,1,0:T(2,128)(2,1)S(1)}, u32[]{:S(2)}, u32[]{:S(2)}) %all-to-all-start.2) | async-done | bytes 262176 | tf_op jit(solution)/shard_map/all_to_all | solution.py:28
  228.2 1.6 convert_bitcast_fusion.1
  229.8 2.2 copy.33
  232.0 1.7 reshape.87
  233.8 6.7 %fusion.10 = (bf16[16,8,1024]{2,1,0:T(8,128)(2,1)}, f32[16,8,1024]{2,1,0:T(8,128)S(1)}) fusion(f32[1024,1024]{1,0:T(8,128)} %mul.18, bf16[1024,1024]{1,0:T(8,128)(2,1)} %all-gather.2.cloned.1.call-done, f32[16,8,1024]{2,1,0:T(8,128)} %reshape.87, f32[16,8,1024]{2,1,0:T(8,128)} %get-tuple-element.6, bf16[16,8,1024]{2,1,0:T(8,128)(2,1)S(1)} %copy-done.1, ...), kind=kOutput, calls=%fused_computation.19 | convolution fusion | flops 1613496320 | bytes 8393216 | tf_op jit(solution)/shard_map/dot_general | solution.py:38
  240.4 2.6 copy.34
  243.1 2.9 reshape.103
  246.0 15.6 %all_to_all.92 = bf16[32,2,2048]{2,1,0:T(2,128)(2,1)} all-to-all(bf16[32,2,2048]{2,1,0:T(2,128)(2,1)} %reshape.103), channel_id=1, replica_groups=mesh['aa'=16,'ba'=32] {'ba'}, dimensions={0} | all-to-all | bytes 524288 | tf_op jit(solution)/shard_map/all_to_all | solution.py:22
  261.6 2.8 reshape.104
  264.4 3.1 copy.35
  267.5 1.9 copy.41
  270.4 22.1 %all_to_all.93 = bf16[16,2,4096]{2,1,0:T(2,128)(2,1)S(1)} all-to-all(bf16[16,2,4096]{2,1,0:T(2,128)(2,1)S(1)} %reshape.105), channel_id=1, replica_groups=mesh['aa'=16,'ba'=32] {'aa'}, dimensions={0} | all-to-all | bytes 524288 | tf_op jit(solution)/shard_map/all_to_all | solution.py:25
  293.3 1.0 reshape.107
  294.3 19.3 %all_to_all.94 = bf16[32,2,2048]{2,1,0:T(2,128)(2,1)S(1)} all-to-all(bf16[32,2,2048]{2,1,0:T(2,128)(2,1)S(1)} %reshape.107), channel_id=1, replica_groups=mesh['aa'=16,'ba'=32] {'ba'}, dimensions={0} | all-to-all | bytes 524288 | tf_op jit(solution)/shard_map/all_to_all | solution.py:28
  314.1 1.6 convert_bitcast_fusion
  315.7 2.2 copy.38
  317.9 1.7 reshape.89
  319.7 2.0 subtract_divide_fusion
  (25 shorter events, 6.4 us)
Async XLA Ops:
  6.5 140.3 %copy-start = (f32[16,8,1024]{2,1,0:T(8,128)S(1)}, f32[16,8,1024]{2,1,0:T(8,128)}, u32[]{:S(2)}) copy-start(f32[16,8,1024]{2,1,0:T(8,128)} %param.6) | copy-start | bytes 1572868
  6.5 140.3 %all-gather.2.cloned.1.call-start = ((), (), s32[]{:S(2)}) async-start(), calls=%async_computation.6 | async-start | bytes 2228224 | tf_op jit(solution)/shard_map/all_gather | solution.py:51
  205.9 10.7 %copy-start.2 = (f32[32]{0:T(128)S(1)}, f32[32]{0:T(128)}, u32[]{:S(2)}) copy-start(f32[32]{0:T(128)} %param.11) | copy-start | bytes 388
  206.0 10.8 %copy-start.3 = (f32[256]{0:T(256)S(1)}, f32[256]{0:T(256)}, u32[]{:S(2)}) copy-start(f32[256]{0:T(256)} %param.10) | copy-start | bytes 3076
  208.0 19.7 %all-to-all-start.2 = ((bf16[32,2,2048]{2,1,0:T(2,128)(2,1)}), bf16[32,2,2048]{2,1,0:T(2,128)(2,1)S(1)}, u32[]{:S(2)}, u32[]{:S(2)}) async-start(bf16[32,2,2048]{2,1,0:T(2,128)(2,1)} %reshape.101), calls=%async_computation.2 | async-start | bytes 524288 | tf_op jit(solution)/shard_map/all_to_all | solution.py:28
  232.0 1.8 copy-start.1
Sparse Core Ops, SparseCore 0:
  54.5 92.3 all-gather.1
where the time goes:
time: 329 us
  blocking collectives  145 us (44%)
  waiting for transfers between devices  91 us (28%)
  local copies, waits for them, and re-layouts  51.4 us (16%)
  between operations  13.6 us (4%)
  matrix products  13 us (4%)
  starting transfers between devices  8.62 us (3%)
  other arithmetic  5.99 us (2%)
    all_gather x1, waiting for transfers between devices, on_device(): whole = lax.all_gather(partial_rows, 'aa', axis=0, tiled=True)  80.3 us
    all_gather x1, blocking collectives, on_device(): partial_rows = lax.all_gather(ladder, 'ba', axis=1, tiled=True)  47 us
    all_to_all x2, blocking collectives, mirrored(): lax.all_to_all(moved.astype(jnp.bfloat16), 'aa', split_axis=1, concat_axi...  45.5 us
    all_to_all x2, blocking collectives, mirrored(): lax.all_to_all(ladder_term.astype(jnp.bfloat16), 'ba', split_axis=2, conc...  33.1 us
    all_to_all x1, blocking collectives, mirrored(): lax.all_to_all(moved.astype(jnp.bfloat16), 'ba', split_axis=0, concat_axi...  19.3 us
    unnamed x20, local copies, waits for them, and re-layouts  16 us
    dot_general x2, matrix products, product(): jnp.dot(field.reshape(rows_a * cols_b, pairs), matrix, precision=lax.Prec...  13 us
    mul x2, local copies, waits for them, and re-layouts, on_device(): whole.astype(jnp.float32).reshape(blocks, BLOCK, blocks, BLOCK) * kept  11.4 us
  transfers between devices with their start and end apart: 2, of which 2 were waited for; matrix products, arithmetic and copies ran while one was open for 4% of the time, Pallas kernels for 0%

commit v1 on v0

v1 whole, which is shorter than its diff:
```python
import functools

import jax
import jax.numpy as jnp
from jax import lax
from jax.experimental import pallas as pl
from jax.experimental.pallas import tpu as pltpu
from jax.sharding import PartitionSpec as P

MESH = pl.DeviceIdType.MESH
F32 = jnp.float32
BF16 = jnp.bfloat16
O = 32
NX = 4
NH = 4
NZ = 16
IJ = 1024
ROWS = 128
COLS = 256
LAG1 = 5
LAG2 = 10


def iota(shape, dim):
    return lax.broadcasted_iota(jnp.int32, shape, dim)


def onehot(cond):
    return jnp.where(cond, 1.0, 0.0).astype(BF16)


def dot(a, b):
    return jnp.dot(a, b, preferred_element_type=F32)


def kernel(
    amp, drv, lad, mask, ve, oe, out,
    G, W, perm, shuf, blk, rden, ab, tb, lhs, x1, x2b, zsend, zrecv, vs,
    z_ss, z_rs, f_ss, f_rs, s_ss, s_rs, c_ss, c_rs, e_ss, e_rs,
):
    p = lax.axis_index("aa")
    q = lax.axis_index("ba")
    zh, x = lax.div(p, NX), lax.rem(p, NX)
    zl = lax.div(q, 2 * NX)
    y = lax.rem(lax.div(q, 2), NX)
    k = lax.rem(q, 2)
    z = zh * NH + zl

    def dev(z_, x_, y_, k_):
        return (lax.div(z_, NH) * NX + x_, lax.rem(z_, NH) * (2 * NX) + y_ * 2 + k_)

    def rot(v, d, n):
        return lax.rem(v + d, n)

    x_peers = [dev(z, rot(x, d, NX), y, k) for d in (1, 3, 2)]
    y_peers = [dev(z, x, rot(y, d, NX), k) for d in (1, 3, 2)]
    sibling = dev(z, x, y, 1 - k)
    z_peer = {d: dev(rot(z, d, NZ), x, y, k) for d in range(1, NZ)}

    barrier = pltpu.get_barrier_semaphore()
    order = [8, 7, 9, 6, 10, 5, 11, 4, 12, 3, 13, 2, 14, 1, 15]
    peers = [z_peer[d] for d in order] + x_peers + y_peers + [sibling]
    for peer in peers:
        pl.semaphore_signal(barrier, inc=1, device_id=peer, device_id_type=MESH)

    keep = mask[p, lax.div(q, 2)].astype(F32)
    packed = jnp.zeros((16, 128), F32)
    for t in range(4):
        place = onehot(iota((32, 128), 1) == iota((32, 128), 0) + 32 * t)
        packed = packed + dot(lad[16 * t : 16 * t + 16, :], place)
    blk[...] = (packed * keep).astype(BF16)
    G[zh, zl, x, y, k] = blk[...]

    def prepare():
        @pl.loop(0, 8)
        def _(i):
            r = iota((128, IJ), 0) + i * 128
            c = iota((128, IJ), 1)
            perm[pl.ds(pl.multiple_of(i * 128, 128), 128), :] = onehot(
                r == (c & (O - 1)) * O + (c >> 5)
            )

        r = iota((512, 512), 0)
        c = iota((512, 512), 1)
        shuf[...] = onehot(c == ((r >> 5) & 3) * 128 + (r >> 7) * 32 + (r & 31))

        lane = iota((8, IJ), 1)
        pair = jnp.zeros((8, IJ), F32)
        for i in range(O):
            e = oe[i]
            pair = pair + jnp.where((lane >> 5) == i, e, 0.0) + jnp.where((lane & (O - 1)) == i, e, 0.0)
        row = iota((8, IJ), 0)
        base = -pair
        for b in range(8):
            base = base + jnp.where(row == b, ve[q * 8 + b], 0.0)
        for a in range(16):
            rden[8 * a : 8 * a + 8, :] = 1.0 / (base + ve[p * 16 + a])
        ab[...] = amp[...].reshape(ROWS, IJ).astype(BF16)

    prepare()
    pl.semaphore_wait(barrier, len(peers))

    def copy(src, dst, ss, rs, to):
        return pltpu.make_async_remote_copy(
            src_ref=src, dst_ref=dst, send_sem=ss, recv_sem=rs, device_id=to, device_id_type=MESH
        )

    def wait_bytes(ref, sem):
        pltpu.make_async_copy(ref, ref, sem).wait()

    for d in order:
        copy(blk, G.at[zh, zl, x, y, k], z_ss.at[d], z_rs.at[d], z_peer[d]).start()

    groups = [0]
    for d in range(1, 8):
        groups += [d, NZ - d]
    groups += [8]

    def first(n):
        e = groups[n]
        src_z = rot(z, NZ - e, NZ)
        h_, l_ = lax.div(src_z, NH), lax.rem(src_z, NH)
        if e:
            wait_bytes(blk, z_rs.at[e])
        piece = G.at[h_, l_, x, y, k]
        for to in x_peers if n % 2 == 0 else y_peers:
            copy(piece, piece, f_ss, f_rs.at[n], to).start()

    def second(n):
        e = groups[n]
        src_z = rot(z, NZ - e, NZ)
        h_, l_ = lax.div(src_z, NH), lax.rem(src_z, NH)
        wait_bytes(G.at[0, 0, 0:3, 0, 0], f_rs.at[n])
        if n % 2 == 0:
            piece, to_all = G.at[h_, l_, :, y, k], y_peers
        else:
            piece, to_all = G.at[h_, l_, x, :, k], x_peers
        for to in to_all:
            copy(piece, piece, s_ss, s_rs.at[n], to).start()

    def third(n):
        e = groups[n]
        src_z = rot(z, NZ - e, NZ)
        h_, l_ = lax.div(src_z, NH), lax.rem(src_z, NH)
        wait_bytes(G.at[0, 0, 0:3, :, 0], s_rs.at[n])
        piece = G.at[h_, l_, :, :, k]
        copy(piece, piece, c_ss, c_rs.at[n], sibling).start()

    for step in range(NZ + LAG2):
        if step < NZ:
            first(step)
        if 0 <= step - LAG1 < NZ:
            second(step - LAG1)
        if 0 <= step - LAG2 < NZ:
            third(step - LAG2)
    for n in range(NZ):
        wait_bytes(G.at[0, 0, :, :, 0], c_rs.at[n])

    @pl.loop(0, 8)
    def _(g):
        l_ = lax.div(g, 2)
        y0 = lax.rem(g, 2) * 2
        wide = jnp.concatenate(
            [G[:, l_, :, y0 + j // 2, j % 2].reshape(256, 128) for j in range(4)], axis=1
        )
        moved = dot(wide, shuf[...]).astype(BF16)
        for t in range(4):
            W[:, t, :, pl.ds(pl.multiple_of(g * 128, 128), 128)] = moved[
                :, 128 * t : 128 * t + 128
            ].reshape(16, 16, 128)

    def columns(n):
        return pl.ds(pl.multiple_of(n * COLS, COLS), COLS)

    def w_cols(n):
        return W[:, :, :, columns(n)].reshape(IJ, COLS)

    @pl.loop(0, IJ // COLS)
    def _(n):
        t1 = dot(ab[...], w_cols(n))
        tb[:, columns(n)] = t1.astype(BF16)
        d = drv[:, :, columns(n)].astype(F32).reshape(ROWS, COLS)
        b1 = (d + t1) * rden[:, columns(n)]
        high = b1.astype(BF16)
        lhs[0:ROWS, columns(n)] = high
        lhs[ROWS : 2 * ROWS, columns(n)] = (b1 - high.astype(F32)).astype(BF16)

    @pl.loop(0, IJ // COLS)
    def _(n):
        turned = dot(tb[...], perm[:, columns(n)]) * rden[:, columns(n)]
        lhs[2 * ROWS : 3 * ROWS, columns(n)] = turned.astype(BF16)

    @pl.loop(0, IJ // COLS)
    def _(n):
        both = dot(lhs[...], w_cols(n))
        x1[:, columns(n)] = both[0:ROWS] + both[ROWS : 2 * ROWS]
        x2b[:, columns(n)] = both[2 * ROWS :].astype(BF16)

    @pl.loop(0, IJ // COLS)
    def _(n):
        zz = x1[:, columns(n)] + dot(x2b[...], perm[:, columns(n)])
        d = drv[:, :, columns(n)].astype(F32).reshape(ROWS, COLS)
        x1[:, columns(n)] = d + zz
        zb = zz.astype(BF16)
        zsend[0, :, columns(n)] = zb[0:64]
        zsend[1, :, columns(n)] = zb[64:128]

    sends = []
    for h in range(2):
        to = (lax.div(q, 2), 2 * p + h)
        own = jnp.logical_and(to[0] == p, to[1] == q)
        sends.append((copy(zsend.at[h], zrecv.at[k], e_ss.at[h], e_rs.at[k], to), own))

        @pl.when(jnp.logical_not(own))
        def _():
            sends[h][0].start()

        @pl.when(own)
        def _():
            pltpu.make_async_copy(zsend.at[h], zrecv.at[k], e_rs.at[k]).start()

    for s in range(2):
        wait_bytes(zrecv.at[s], e_rs.at[s])

        @pl.loop(0, IJ // COLS)
        def _(n):
            turned = dot(zrecv[s], perm[:, columns(n)])
            for c in range(COLS // 128):
                vs[c] = turned[:, 128 * c : 128 * c + 128]
            for b in range(8):
                r = 8 * (8 * s + b)
                other = jnp.concatenate(
                    [vs[c, pl.ds(b, 8, stride=8), :] for c in range(COLS // 128)], axis=1
                )
                out[8 * s + b, :, columns(n)] = (
                    x1[r : r + 8, columns(n)] + other
                ) * rden[r : r + 8, columns(n)]

    for d in order:
        wait_bytes(blk, z_ss.at[d])
    wait_bytes(G.at[0:3, :, :, 0, 0], f_ss)
    wait_bytes(G.at[0:3, :, :, :, 0], s_ss)
    wait_bytes(G.at[:, :, :, :, 0], c_ss)
    for h in range(2):

        @pl.when(jnp.logical_not(sends[h][1]))
        def _():
            sends[h][0].wait_send()


def on_device(amplitudes, driving, ladder, block_mask, virt_energy, occ_energy):
    vmem = pl.BlockSpec(memory_space=pltpu.VMEM)
    smem = pl.BlockSpec(memory_space=pltpu.SMEM)
    dma = pltpu.SemaphoreType.DMA
    return pl.pallas_call(
        kernel,
        out_shape=jax.ShapeDtypeStruct(amplitudes.shape, F32),
        in_specs=[vmem, vmem, vmem, smem, smem, smem],
        out_specs=vmem,
        scratch_shapes=[
            pltpu.VMEM((NH, NH, NX, NX, 2, 16, 128), BF16),
            pltpu.VMEM((16, 4, 16, IJ), BF16),
            pltpu.VMEM((IJ, IJ), BF16),
            pltpu.VMEM((512, 512), BF16),
            pltpu.VMEM((16, 128), BF16),
            pltpu.VMEM((ROWS, IJ), F32),
            pltpu.VMEM((ROWS, IJ), BF16),
            pltpu.VMEM((ROWS, IJ), BF16),
            pltpu.VMEM((3 * ROWS, IJ), BF16),
            pltpu.VMEM((ROWS, IJ), F32),
            pltpu.VMEM((ROWS, IJ), BF16),
            pltpu.VMEM((2, 64, IJ), BF16),
            pltpu.VMEM((2, 64, IJ), BF16),
            pltpu.VMEM((COLS // 128, 64, 128), F32),
            dma((NZ,)),
            dma((NZ,)),
            dma(()),
            dma((NZ,)),
            dma(()),
            dma((NZ,)),
            dma(()),
            dma((NZ,)),
            dma((2,)),
            dma((2,)),
        ],
        compiler_params=pltpu.CompilerParams(collective_id=0, has_side_effects=True),
    )(amplitudes, driving, ladder, block_mask, virt_energy, occ_energy)


def solution(mesh):
    placed = (P("aa", "ba", None), P("aa", "ba", None), P("aa", "ba"), P(), P(), P())
    return jax.shard_map(
        on_device, mesh=mesh, in_specs=placed, out_specs=P("aa", "ba", None), check_vma=False
    )
```

time: 329 us -> 75 us (0.23)
  the two profiles are of different devices: /device:TPU:1 before, /device:TPU:81 now
where the time goes in v1:
time: 75 us; the launch traced here: 74.8 us
  Pallas kernels  71.5 us (95%)
  local copies, waits for them, and re-layouts  3.27 us (4%)
    pallas_call x1, Pallas kernels, on_device(): pl.pallas_call(kernel, out_shape=jax.ShapeDtypeStruct(amplitudes.shape, F...  71.5 us
    unnamed x2, local copies, waits for them, and re-layouts  3.27 us

profile of v1, /device:TPU:81, one launch (start us, length us, event | category | flops | bytes accessed | tf_op | source)
XLA Modules:
  0.0 74.8 jit_solution(11672470701269589670)
XLA Ops:
  0.0 1.4 %copy.7.lad = bf16[64,32]{1,0:T(8,128)(2,1)} copy(bf16[64,32]{0,1:T(8,128)(2,1)} %param.8) | data formatting | bytes 8192 | tf_op args[2]
  1.4 71.5 %shard_map.64 = f32[16,8,1024]{2,1,0:T(8,128)} custom-call(f32[16,8,1024]{2,1,0:T(8,128)} %amp.1, bf16[16,8,1024]{2,1,0:T(8,128)(2,1)} %drv.1, bf16[64,32]{1,0:T(8,128)(2,1)} %copy.7.lad, s32[16,16]{1,0:T(8,128)} %mask.1, f32[256]{0:T(256)} %ve.1, f32[32]{0:T(128)} %oe.1), custom_call_target="tpu_custom_call" | custom-call | tf_op jit(solution)/shard_map/pallas_call | solution.py:255
  72.9 1.9 %copy.9 = f32[16,8,1024]{2,1,0:T(8,128)} copy(f32[16,8,1024]{2,1,0:T(8,128)} %shard_map.64) | data formatting | bytes 1048576

commit v2 on v1

v2 whole, which is shorter than its diff:
```python
import jax
import jax.numpy as jnp
from jax import lax
from jax.experimental import pallas as pl
from jax.experimental.pallas import tpu as pltpu
from jax.sharding import PartitionSpec as P

MESH = pl.DeviceIdType.MESH
F32 = jnp.float32
BF16 = jnp.bfloat16
O = 32
NX = 4
NH = 4
NZ = 16
IJ = 1024
ROWS = 128
COLS = 256
CHUNKS = IJ // COLS
NEAR = (1, 15, 2, 14, 3, 13, 4, 12)
GROUPS = (0,) + NEAR + (5, 11, 6, 10, 7, 9, 8)
HOP, BASE = 0.78, 0.88


def arrival(e):
    d = min(e, NZ - e)
    if d == 0:
        return 0.0
    return BASE + HOP * d if d <= 4 else 2 * BASE + HOP * d


def plan():
    events = []
    for n, e in enumerate(GROUPS):
        t = arrival(e)
        events += [(t, 0, n), (t + 2.5, 1, n), (t + 5.0, 2, n), (t + 6.6, 3, n)]
    return [(kind, n) for _, kind, n in sorted(events)]


def iota(shape, dim):
    return lax.broadcasted_iota(jnp.int32, shape, dim)


def onehot(cond):
    return jnp.where(cond, 1.0, 0.0).astype(BF16)


def dot(a, b):
    return jnp.dot(a, b, preferred_element_type=F32)


def kernel(
    amp_hbm, drv_hbm, lad, mask, ve, oe, out,
    G, W, perm, shuf, blk, amp, drv, rden, ab, tacc, tb, lhs, x1, x2b, zsend, zrecv, vs,
    in_s, z_ss, z_rs, f_ss, f_rs, s_ss, s_rs, c_ss, c_rs, e_ss, e_rs,
):
    p = lax.axis_index("aa")
    q = lax.axis_index("ba")
    zh, x = lax.div(p, NX), lax.rem(p, NX)
    zl = lax.div(q, 2 * NX)
    y = lax.rem(lax.div(q, 2), NX)
    k = lax.rem(q, 2)
    z = zh * NH + zl

    def dev(z_, x_, y_, k_):
        return (lax.div(z_, NH) * NX + x_, lax.rem(z_, NH) * (2 * NX) + y_ * 2 + k_)

    def rot(v, d, n):
        return lax.rem(v + d, n)

    x_peers = [dev(z, rot(x, d, NX), y, k) for d in (2, 1, 3)]
    y_peers = [dev(z, x, rot(y, d, NX), k) for d in (2, 1, 3)]
    sibling = dev(z, x, y, 1 - k)
    z_peer = {d: dev(rot(z, d, NZ), x, y, k) for d in NEAR}

    barrier = pltpu.get_barrier_semaphore()
    peers = [z_peer[d] for d in reversed(NEAR)] + x_peers + y_peers + [sibling]
    for peer in peers:
        pl.semaphore_signal(barrier, inc=1, device_id=peer, device_id_type=MESH)

    loads = [
        pltpu.make_async_copy(amp_hbm, amp, in_s.at[0]),
        pltpu.make_async_copy(drv_hbm, drv, in_s.at[1]),
    ]
    for load in loads:
        load.start()

    keep = mask[p, lax.div(q, 2)].astype(F32)
    eye = onehot(iota((64, 64), 0) == iota((64, 64), 1))
    rows = lax.dot_general(
        eye, lad[...], (((1,), (1,)), ((), ())), preferred_element_type=F32
    ).astype(BF16)
    packed = jnp.zeros((16, 128), F32)
    for t in range(4):
        place = onehot(iota((32, 128), 1) == iota((32, 128), 0) + 32 * t)
        packed = packed + dot(rows[16 * t : 16 * t + 16, :], place)
    packed = (packed * keep).astype(BF16)
    blk[...] = packed
    G[zh, zl, k, x, y] = packed

    def copy(src, dst, ss, rs, to):
        return pltpu.make_async_remote_copy(
            src_ref=src, dst_ref=dst, send_sem=ss, recv_sem=rs, device_id=to, device_id_type=MESH
        )

    def wait_bytes(ref, sem):
        pltpu.make_async_copy(ref, ref, sem).wait()

    pl.semaphore_wait(barrier, len(peers))
    for d in reversed(NEAR):
        copy(blk, G.at[zh, zl, k, x, y], z_ss.at[d], z_rs.at[d], z_peer[d]).start()

    def plane(e):
        src_z = rot(z, NZ - e, NZ)
        return lax.div(src_z, NH), lax.rem(src_z, NH)

    def first(n):
        e = GROUPS[n]
        h_, l_ = plane(e)
        piece = G.at[h_, l_, k, x, y]
        if e:
            wait_bytes(blk, z_rs.at[e])
        if 1 <= e <= 4:
            copy(piece, piece, z_ss.at[e + 4], z_rs.at[e + 4], z_peer[4]).start()
        if 13 <= e <= 15:
            copy(piece, piece, z_ss.at[e - 4], z_rs.at[e - 4], z_peer[12]).start()
        for to in x_peers if n % 2 == 0 else y_peers:
            copy(piece, piece, f_ss, f_rs.at[n], to).start()

    def second(n):
        h_, l_ = plane(GROUPS[n])
        wait_bytes(G.at[0, 0, 0, 0, 0:3], f_rs.at[n])
        if n % 2 == 0:
            piece, to_all = G.at[h_, l_, k, :, y], y_peers
        else:
            piece, to_all = G.at[h_, l_, k, x], x_peers
        for to in to_all:
            copy(piece, piece, s_ss, s_rs.at[n], to).start()

    def third(n):
        h_, l_ = plane(GROUPS[n])
        wait_bytes(G.at[0, 0, 0, 0:3], s_rs.at[n])
        piece = G.at[h_, l_, k]
        copy(piece, piece, c_ss, c_rs.at[n], sibling).start()

    def use(n):
        h_, l_ = plane(GROUPS[n])
        wait_bytes(G.at[0, 0, 0], c_rs.at[n])
        wide = jnp.concatenate(
            [
                jnp.concatenate(
                    [G[h_, l_, j % 2, :, 2 * g + j // 2].reshape(64, 128) for j in range(4)], axis=1
                )
                for g in range(2)
            ],
            axis=0,
        )
        moved = dot(wide, shuf[...]).astype(BF16)
        cols = pl.ds(pl.multiple_of(l_ * COLS, COLS), COLS)
        for t in range(4):
            W[pl.ds(h_ * NX, NX), t, :, cols] = jnp.concatenate(
                [moved[64 * g : 64 * g + 64, 128 * t : 128 * t + 128] for g in range(2)], axis=1
            ).reshape(NX, 16, COLS)
        block = W[pl.ds(h_ * NX, NX), :, :, cols].reshape(COLS, COLS)
        tacc[:, cols] += dot(ab[:, pl.ds(pl.multiple_of(h_ * COLS, COLS), COLS)], block)

    def prepare():
        r = iota((512, 512), 0)
        c = iota((512, 512), 1)
        shuf[...] = onehot(c == ((r >> 5) & 3) * 128 + (r >> 7) * 32 + (r & 31))
        tacc[...] = jnp.zeros((ROWS, IJ), F32)
        loads[0].wait()
        ab[...] = amp[...].reshape(ROWS, IJ).astype(BF16)

        @pl.loop(0, 8)
        def _(i):
            r = iota((128, IJ), 0) + i * 128
            c = iota((128, IJ), 1)
            perm[pl.ds(pl.multiple_of(i * 128, 128), 128), :] = onehot(
                r == (c & (O - 1)) * O + (c >> 5)
            )

        lane = iota((8, IJ), 1)
        pair = jnp.zeros((8, IJ), F32)
        for i in range(O):
            e = oe[i]
            pair = pair + jnp.where((lane >> 5) == i, e, 0.0) + jnp.where((lane & (O - 1)) == i, e, 0.0)
        row = iota((8, IJ), 0)
        base = -pair
        for b in range(8):
            base = base + jnp.where(row == b, ve[q * 8 + b], 0.0)
        for a in range(16):
            rden[8 * a : 8 * a + 8, :] = 1.0 / (base + ve[p * 16 + a])
        loads[1].wait()

    steps = [first, second, third, use]
    for i, (kind, n) in enumerate(plan()):
        if i == 1:
            prepare()
        steps[kind](n)

    def columns(n):
        return pl.ds(pl.multiple_of(n * COLS, COLS), COLS)

    def w_cols(n):
        return W[:, :, :, columns(n)].reshape(IJ, COLS)

    def wide_driving(n):
        return drv[:, :, columns(n)].astype(F32).reshape(ROWS, COLS)

    @pl.loop(0, CHUNKS)
    def _(n):
        t1 = tacc[:, columns(n)]
        tb[:, columns(n)] = t1.astype(BF16)
        b1 = (wide_driving(n) + t1) * rden[:, columns(n)]
        high = b1.astype(BF16)
        lhs[0:ROWS, columns(n)] = high
        lhs[ROWS : 2 * ROWS, columns(n)] = (b1 - high.astype(F32)).astype(BF16)

    @pl.loop(0, CHUNKS)
    def _(n):
        turned = dot(tb[...], perm[:, columns(n)]) * rden[:, columns(n)]
        lhs[2 * ROWS : 3 * ROWS, columns(n)] = turned.astype(BF16)

    @pl.loop(0, CHUNKS)
    def _(n):
        both = dot(lhs[...], w_cols(n))
        x1[:, columns(n)] = both[0:ROWS] + both[ROWS : 2 * ROWS]
        x2b[:, columns(n)] = both[2 * ROWS :].astype(BF16)

    def to_half(h):
        to = (lax.div(q, 2), 2 * p + h)
        return to, jnp.logical_and(to[0] == p, to[1] == q)

    def exchange(n, h):
        to, own = to_half(h)
        return copy(zsend.at[n, h], zrecv.at[n, k], e_ss.at[n, h], e_rs.at[n, k], to), own

    for n in range(CHUNKS):
        cols = slice(n * COLS, (n + 1) * COLS)
        zz = x1[:, cols] + dot(x2b[...], perm[:, cols])
        x1[:, cols] = drv[:, :, cols].astype(F32).reshape(ROWS, COLS) + zz
        zsend[n] = zz.astype(BF16).reshape(2, 64, COLS)
        for h in range(2):
            send, own = exchange(n, h)

            @pl.when(jnp.logical_not(own))
            def _():
                send.start()

            @pl.when(own)
            def _():
                pltpu.make_async_copy(zsend.at[n, h], zrecv.at[n, k], e_rs.at[n, k]).start()

    for n in range(CHUNKS):
        for s in range(2):
            wait_bytes(zrecv.at[n, s], e_rs.at[n, s])
        got = zrecv[n].reshape(ROWS, COLS)
        for m in range(CHUNKS):
            turned = dot(got, perm[n * COLS : (n + 1) * COLS, m * COLS : (m + 1) * COLS])
            for c in range(COLS // 128):
                part = turned[:, 128 * c : 128 * c + 128]
                if n:
                    vs[m * (COLS // 128) + c] += part
                else:
                    vs[m * (COLS // 128) + c] = part

    @pl.loop(0, IJ // 128)
    def _(c):
        cols = pl.ds(pl.multiple_of(c * 128, 128), 128)
        for s in range(2):
            for b in range(8):
                r = 8 * (8 * s + b)
                other = vs[c, pl.ds(64 * s + b, 8, stride=8), :]
                out[8 * s + b, :, cols] = (x1[r : r + 8, cols] + other) * rden[r : r + 8, cols]

    for d in NEAR + GROUPS[9:]:
        wait_bytes(blk, z_ss.at[d])
    wait_bytes(G.at[0:3, :, 0, :, 0], f_ss)
    wait_bytes(G.at[0:3, :, 0], s_ss)
    wait_bytes(G.at[:, :, 0], c_ss)
    for n in range(CHUNKS):
        for h in range(2):
            send, own = exchange(n, h)

            @pl.when(jnp.logical_not(own))
            def _():
                send.wait_send()


def on_device(amplitudes, driving, ladder, block_mask, virt_energy, occ_energy):
    vmem = pl.BlockSpec(memory_space=pltpu.VMEM)
    smem = pl.BlockSpec(memory_space=pltpu.SMEM)
    hbm = pl.BlockSpec(memory_space=pltpu.HBM)
    dma = pltpu.SemaphoreType.DMA
    return pl.pallas_call(
        kernel,
        out_shape=jax.ShapeDtypeStruct(amplitudes.shape, F32),
        in_specs=[hbm, hbm, vmem, smem, smem, smem],
        out_specs=vmem,
        scratch_shapes=[
            pltpu.VMEM((NH, NH, 2, NX, NX, 16, 128), BF16),
            pltpu.VMEM((16, 4, 16, IJ), BF16),
            pltpu.VMEM((IJ, IJ), BF16),
            pltpu.VMEM((512, 512), BF16),
            pltpu.VMEM((16, 128), BF16),
            pltpu.VMEM(amplitudes.shape, F32),
            pltpu.VMEM(driving.shape, BF16),
            pltpu.VMEM((ROWS, IJ), F32),
            pltpu.VMEM((ROWS, IJ), BF16),
            pltpu.VMEM((ROWS, IJ), F32),
            pltpu.VMEM((ROWS, IJ), BF16),
            pltpu.VMEM((3 * ROWS, IJ), BF16),
            pltpu.VMEM((ROWS, IJ), F32),
            pltpu.VMEM((ROWS, IJ), BF16),
            pltpu.VMEM((CHUNKS, 2, 64, COLS), BF16),
            pltpu.VMEM((CHUNKS, 2, 64, COLS), BF16),
            pltpu.VMEM((IJ // 128, ROWS, 128), F32),
            dma((2,)),
            dma((NZ,)),
            dma((NZ,)),
            dma(()),
            dma((NZ,)),
            dma(()),
            dma((NZ,)),
            dma(()),
            dma((NZ,)),
            dma((CHUNKS, 2)),
            dma((CHUNKS, 2)),
        ],
        compiler_params=pltpu.CompilerParams(collective_id=0, has_side_effects=True),
    )(amplitudes, driving, ladder.T, block_mask, virt_energy, occ_energy)


def solution(mesh):
    placed = (P("aa", "ba", None), P("aa", "ba", None), P("aa", "ba"), P(), P(), P())
    return jax.shard_map(
        on_device, mesh=mesh, in_specs=placed, out_specs=P("aa", "ba", None), check_vma=False
    )
```

time: 75 us -> 65.5 us (0.87)
  the two profiles are of different devices: /device:TPU:81 before, /device:TPU:101 now
where the time goes in v2:
time: 65.5 us; the launch traced here: 65.3 us
  Pallas kernels  63.4 us (97%)
  local copies, waits for them, and re-layouts  1.89 us (3%)
    pallas_call x1, Pallas kernels, on_device(): pl.pallas_call(kernel, out_shape=jax.ShapeDtypeStruct(amplitudes.shape, F...  63.4 us
    unnamed x1, local copies, waits for them, and re-layouts  1.89 us

profile of v2, /device:TPU:101, one launch (start us, length us, event | category | flops | bytes accessed | tf_op | source)
XLA Modules:
  0.0 65.3 jit_solution(15349671785248513900)
XLA Ops:
  0.0 63.4 %shard_map.64 = f32[16,8,1024]{2,1,0:T(8,128)} custom-call(f32[16,8,1024]{2,1,0:T(8,128)} %amp_hbm.1, bf16[16,8,1024]{2,1,0:T(8,128)(2,1)} %drv_hbm.1, bf16[32,64]{1,0:T(8,128)(2,1)} %bitcast.1, s32[16,16]{1,0:T(8,128)} %mask.1, f32[256]{0:T(256)} %ve.1, f32[32]{0:T(128)} %oe.1), custom_call_target="tpu_custom_call" | custom-call | tf_op jit(solution)/shard_map/pallas_call | solution.py:295
  63.5 1.9 %copy.8 = f32[16,8,1024]{2,1,0:T(8,128)} copy(f32[16,8,1024]{2,1,0:T(8,128)} %shard_map.64) | data formatting | bytes 1048576

commit v3 on v2

--- a/solution.py
+++ b/solution.py
@@ -18,22 +18,22 @@
 CHUNKS = IJ // COLS
 NEAR = (1, 15, 2, 14, 3, 13, 4, 12)
 GROUPS = (0,) + NEAR + (5, 11, 6, 10, 7, 9, 8)
-HOP, BASE = 0.78, 0.88
-
-
-def arrival(e):
-    d = min(e, NZ - e)
-    if d == 0:
-        return 0.0
-    return BASE + HOP * d if d <= 4 else 2 * BASE + HOP * d
+EARLY = 3
+EROWS = 2 * EARLY * 8
+LAG = 4
+RAW_AT = 0
 
 
 def plan():
-    events = []
-    for n, e in enumerate(GROUPS):
-        t = arrival(e)
-        events += [(t, 0, n), (t + 2.5, 1, n), (t + 5.0, 2, n), (t + 6.6, 3, n)]
-    return [(kind, n) for _, kind, n in sorted(events)]
+    events = [(0, n) for n in range(NZ)] + [(1, n) for n in range(NZ)]
+    for n in range(NZ + LAG):
+        if n == RAW_AT:
+            events.append((4, 0))
+        if n < NZ:
+            events.append((2, n))
+        if n >= LAG:
+            events.append((3, n - LAG))
+    return events
 
 
 def iota(shape, dim):
@@ -50,8 +50,8 @@
 
 def kernel(
     amp_hbm, drv_hbm, lad, mask, ve, oe, out,
-    G, W, perm, shuf, blk, amp, drv, rden, ab, tacc, tb, lhs, x1, x2b, zsend, zrecv, vs,
-    in_s, z_ss, z_rs, f_ss, f_rs, s_ss, s_rs, c_ss, c_rs, e_ss, e_rs,
+    G, W, perm, shuf, blk, amp, drv, abt, rden, ab, tb, lhs, x1, x2b, zsend, zrecv, vs,
+    araw, draw, rden2, ab2, tb2, lhs2, x12, x2b2, in_s, r_ss, r_rs, z_ss, z_rs, f_ss, f_rs, s_ss, s_rs, c_ss, c_rs, e_ss, e_rs,
 ):
     p = lax.axis_index("aa")
     q = lax.axis_index("ba")
@@ -74,6 +74,8 @@
 
     barrier = pltpu.get_barrier_semaphore()
     peers = [z_peer[d] for d in reversed(NEAR)] + x_peers + y_peers + [sibling]
+    peers += [dev(z, rot(x, d, NX), y, 1 - k) for d in (2, 1, 3)]
+    peers += [dev(z, x, rot(y, d, NX), 1 - k) for d in (2, 1, 3)]
     for peer in peers:
         pl.semaphore_signal(barrier, inc=1, device_id=peer, device_id_type=MESH)
 
@@ -160,16 +162,14 @@
             W[pl.ds(h_ * NX, NX), t, :, cols] = jnp.concatenate(
                 [moved[64 * g : 64 * g + 64, 128 * t : 128 * t + 128] for g in range(2)], axis=1
             ).reshape(NX, 16, COLS)
-        block = W[pl.ds(h_ * NX, NX), :, :, cols].reshape(COLS, COLS)
-        tacc[:, cols] += dot(ab[:, pl.ds(pl.multiple_of(h_ * COLS, COLS), COLS)], block)
 
     def prepare():
         r = iota((512, 512), 0)
         c = iota((512, 512), 1)
         shuf[...] = onehot(c == ((r >> 5) & 3) * 128 + (r >> 7) * 32 + (r & 31))
-        tacc[...] = jnp.zeros((ROWS, IJ), F32)
         loads[0].wait()
         ab[...] = amp[...].reshape(ROWS, IJ).astype(BF16)
+        abt[...] = amp[...].astype(BF16)
 
         @pl.loop(0, 8)
         def _(i):
@@ -185,14 +185,52 @@
             e = oe[i]
             pair = pair + jnp.where((lane >> 5) == i, e, 0.0) + jnp.where((lane & (O - 1)) == i, e, 0.0)
         row = iota((8, IJ), 0)
-        base = -pair
-        for b in range(8):
-            base = base + jnp.where(row == b, ve[q * 8 + b], 0.0)
+
+        def over(first_b):
+            base = -pair
+            for b in range(8):
+                base = base + jnp.where(row == b, ve[first_b + b], 0.0)
+            return base
+
+        base = over(q * 8)
         for a in range(16):
             rden[8 * a : 8 * a + 8, :] = 1.0 / (base + ve[p * 16 + a])
+        for s in range(2):
+            base = over(p * 16 + 8 * s)
+            for a in range(EARLY):
+                r = 8 * (s * EARLY + a)
+                rden2[r : r + 8, :] = 1.0 / (base + ve[q * 8 + a])
         loads[1].wait()
 
-    steps = [first, second, third, use]
+    def give(src, dst, ss, rs, h):
+        to = (lax.div(q, 2), 2 * p + h)
+        own = jnp.logical_and(to[0] == p, to[1] == q)
+        send = copy(src, dst, ss, rs, to)
+
+        @pl.when(jnp.logical_not(own))
+        def _():
+            send.start()
+
+        @pl.when(own)
+        def _():
+            pltpu.make_async_copy(src, dst, rs).start()
+
+        def done():
+            @pl.when(jnp.logical_not(own))
+            def _():
+                send.wait_send()
+
+        return done
+
+    given = []
+
+    def early(_):
+        for h in range(2):
+            for j, (src, dst) in enumerate(((abt, araw), (drv, draw))):
+                piece = src.at[8 * h : 8 * h + EARLY]
+                given.append(give(piece, dst.at[k], r_ss.at[h, j], r_rs.at[k, j], h))
+
+    steps = [first, second, third, use, early]
     for i, (kind, n) in enumerate(plan()):
         if i == 1:
             prepare()
@@ -204,57 +242,62 @@
     def w_cols(n):
         return W[:, :, :, columns(n)].reshape(IJ, COLS)
 
-    def wide_driving(n):
+    def halves(count, tile, drive, over_den, t_, l_, one, two):
+        @pl.loop(0, CHUNKS)
+        def _(n):
+            t1 = dot(tile[...], w_cols(n))
+            t_[:, columns(n)] = t1.astype(BF16)
+            b1 = (drive(n) + t1) * over_den[:, columns(n)]
+            high = b1.astype(BF16)
+            l_[0:count, columns(n)] = high
+            l_[count : 2 * count, columns(n)] = (b1 - high.astype(F32)).astype(BF16)
+
+        @pl.loop(0, CHUNKS)
+        def _(n):
+            turned = dot(t_[...], perm[:, columns(n)]) * over_den[:, columns(n)]
+            l_[2 * count : 3 * count, columns(n)] = turned.astype(BF16)
+
+        @pl.loop(0, CHUNKS)
+        def _(n):
+            both = dot(l_[...], w_cols(n))
+            one[:, columns(n)] = both[0:count] + both[count : 2 * count]
+            two[:, columns(n)] = both[2 * count :].astype(BF16)
+
+    def drive(n):
         return drv[:, :, columns(n)].astype(F32).reshape(ROWS, COLS)
 
-    @pl.loop(0, CHUNKS)
-    def _(n):
-        t1 = tacc[:, columns(n)]
-        tb[:, columns(n)] = t1.astype(BF16)
-        b1 = (wide_driving(n) + t1) * rden[:, columns(n)]
-        high = b1.astype(BF16)
-        lhs[0:ROWS, columns(n)] = high
-        lhs[ROWS : 2 * ROWS, columns(n)] = (b1 - high.astype(F32)).astype(BF16)
-
-    @pl.loop(0, CHUNKS)
-    def _(n):
-        turned = dot(tb[...], perm[:, columns(n)]) * rden[:, columns(n)]
-        lhs[2 * ROWS : 3 * ROWS, columns(n)] = turned.astype(BF16)
-
-    @pl.loop(0, CHUNKS)
-    def _(n):
-        both = dot(lhs[...], w_cols(n))
-        x1[:, columns(n)] = both[0:ROWS] + both[ROWS : 2 * ROWS]
-        x2b[:, columns(n)] = both[2 * ROWS :].astype(BF16)
-
-    def to_half(h):
-        to = (lax.div(q, 2), 2 * p + h)
-        return to, jnp.logical_and(to[0] == p, to[1] == q)
-
-    def exchange(n, h):
-        to, own = to_half(h)
-        return copy(zsend.at[n, h], zrecv.at[n, k], e_ss.at[n, h], e_rs.at[n, k], to), own
+    halves(ROWS, ab, drive, rden, tb, lhs, x1, x2b)
 
     for n in range(CHUNKS):
         cols = slice(n * COLS, (n + 1) * COLS)
         zz = x1[:, cols] + dot(x2b[...], perm[:, cols])
         x1[:, cols] = drv[:, :, cols].astype(F32).reshape(ROWS, COLS) + zz
-        zsend[n] = zz.astype(BF16).reshape(2, 64, COLS)
+        zsend[n] = zz.reshape(2, 8, 8, COLS).astype(BF16)
         for h in range(2):
-            send, own = exchange(n, h)
-
-            @pl.when(jnp.logical_not(own))
-            def _():
-                send.start()
-
-            @pl.when(own)
-            def _():
-                pltpu.make_async_copy(zsend.at[n, h], zrecv.at[n, k], e_rs.at[n, k]).start()
+            given.append(
+                give(
+                    zsend.at[n, h, EARLY:8], zrecv.at[n, k, EARLY:8], e_ss.at[n, h], e_rs.at[n, k], h
+                )
+            )
+
+    for s in range(2):
+        for j, dst in enumerate((araw, draw)):
+            wait_bytes(dst.at[s], r_rs.at[s, j])
+    ab2[...] = araw[...].astype(F32).reshape(EROWS, IJ).astype(BF16)
+
+    def early_drive(n):
+        return draw[:, :, :, columns(n)].astype(F32).reshape(EROWS, COLS)
+
+    halves(EROWS, ab2, early_drive, rden2, tb2, lhs2, x12, x2b2)
+    for n in range(CHUNKS):
+        cols = slice(n * COLS, (n + 1) * COLS)
+        zz = x12[:, cols] + dot(x2b2[...], perm[:, cols])
+        zrecv[n, :, 0:EARLY] = zz.reshape(2, EARLY, 8, COLS).astype(BF16)
 
     for n in range(CHUNKS):
         for s in range(2):
-            wait_bytes(zrecv.at[n, s], e_rs.at[n, s])
-        got = zrecv[n].reshape(ROWS, COLS)
+            wait_bytes(zrecv.at[n, s, EARLY:8], e_rs.at[n, s])
+        got = zrecv[n].astype(F32).reshape(ROWS, COLS).astype(BF16)
         for m in range(CHUNKS):
             turned = dot(got, perm[n * COLS : (n + 1) * COLS, m * COLS : (m + 1) * COLS])
             for c in range(COLS // 128):
@@ -278,13 +321,8 @@
     wait_bytes(G.at[0:3, :, 0, :, 0], f_ss)
     wait_bytes(G.at[0:3, :, 0], s_ss)
     wait_bytes(G.at[:, :, 0], c_ss)
-    for n in range(CHUNKS):
-        for h in range(2):
-            send, own = exchange(n, h)
-
-            @pl.when(jnp.logical_not(own))
-            def _():
-                send.wait_send()
+    for done in given:
+        done()
 
 
 def on_device(amplitudes, driving, ladder, block_mask, virt_energy, occ_energy):
@@ -305,17 +343,27 @@
             pltpu.VMEM((16, 128), BF16),
             pltpu.VMEM(amplitudes.shape, F32),
             pltpu.VMEM(driving.shape, BF16),
+            pltpu.VMEM(amplitudes.shape, BF16),
             pltpu.VMEM((ROWS, IJ), F32),
             pltpu.VMEM((ROWS, IJ), BF16),
-            pltpu.VMEM((ROWS, IJ), F32),
             pltpu.VMEM((ROWS, IJ), BF16),
             pltpu.VMEM((3 * ROWS, IJ), BF16),
             pltpu.VMEM((ROWS, IJ), F32),
             pltpu.VMEM((ROWS, IJ), BF16),
-            pltpu.VMEM((CHUNKS, 2, 64, COLS), BF16),
-            pltpu.VMEM((CHUNKS, 2, 64, COLS), BF16),
+            pltpu.VMEM((CHUNKS, 2, 8, 8, COLS), BF16),
+            pltpu.VMEM((CHUNKS, 2, 8, 8, COLS), BF16),
             pltpu.VMEM((IJ // 128, ROWS, 128), F32),
+            pltpu.VMEM((2, EARLY, 8, IJ), BF16),
+            pltpu.VMEM((2, EARLY, 8, IJ), BF16),
+            pltpu.VMEM((EROWS, IJ), F32),
+            pltpu.VMEM((EROWS, IJ), BF16),
+            pltpu.VMEM((EROWS, IJ), BF16),
+            pltpu.VMEM((3 * EROWS, IJ), BF16),
+            pltpu.VMEM((EROWS, IJ), F32),
+            pltpu.VMEM((EROWS, IJ), BF16),
             dma((2,)),
+            dma((2, 2)),
+            dma((2, 2)),
             dma((NZ,)),
             dma((NZ,)),
             dma(()),

time: 65.5 us -> 60.5 us (0.924)
  the two profiles are of different devices: /device:TPU:101 before, /device:TPU:49 now
where the time goes in v3:
time: 60.5 us; the launch traced here: 60.3 us
  Pallas kernels  58.4 us (97%)
  local copies, waits for them, and re-layouts  1.89 us (3%)
    pallas_call x1, Pallas kernels, on_device(): pl.pallas_call(kernel, out_shape=jax.ShapeDtypeStruct(amplitudes.shape, F...  58.4 us
    unnamed x1, local copies, waits for them, and re-layouts  1.89 us

profile of v3, /device:TPU:49, one launch (start us, length us, event | category | flops | bytes accessed | tf_op | source)
XLA Modules:
  0.0 60.3 jit_solution(966101609280335163)
XLA Ops:
  0.0 58.4 %shard_map.64 = f32[16,8,1024]{2,1,0:T(8,128)} custom-call(f32[16,8,1024]{2,1,0:T(8,128)} %amp_hbm.1, bf16[16,8,1024]{2,1,0:T(8,128)(2,1)} %drv_hbm.1, bf16[32,64]{1,0:T(8,128)(2,1)} %bitcast.1, s32[16,16]{1,0:T(8,128)} %mask.1, f32[256]{0:T(256)} %ve.1, f32[32]{0:T(128)} %oe.1), custom_call_target="tpu_custom_call" | custom-call | tf_op jit(solution)/shard_map/pallas_call | solution.py:333
  58.4 1.9 %copy.8 = f32[16,8,1024]{2,1,0:T(8,128)} copy(f32[16,8,1024]{2,1,0:T(8,128)} %shard_map.64) | data formatting | bytes 1048576

commit v4 on v3

--- a/solution.py
+++ b/solution.py
@@ -50,8 +50,8 @@
 
 def kernel(
     amp_hbm, drv_hbm, lad, mask, ve, oe, out,
-    G, W, perm, shuf, blk, amp, drv, abt, rden, ab, tb, lhs, x1, x2b, zsend, zrecv, vs,
-    araw, draw, rden2, ab2, tb2, lhs2, x12, x2b2, in_s, r_ss, r_rs, z_ss, z_rs, f_ss, f_rs, s_ss, s_rs, c_ss, c_rs, e_ss, e_rs,
+    G, W, perm, shuf, blk, amp, drv, abt, rden, ab, tb, lhs, cb, x1, x2b, zsend, zrecv, vs,
+    araw, draw, rden2, ab2, tb2, lhs2, cb2, x2b2, in_s, r_ss, r_rs, z_ss, z_rs, f_ss, f_rs, s_ss, s_rs, c_ss, c_rs, e_ss, e_rs,
 ):
     p = lax.axis_index("aa")
     q = lax.axis_index("ba")
@@ -237,40 +237,44 @@
         steps[kind](n)
 
     def columns(n):
+        if isinstance(n, int):
+            return slice(n * COLS, (n + 1) * COLS)
         return pl.ds(pl.multiple_of(n * COLS, COLS), COLS)
 
     def w_cols(n):
         return W[:, :, :, columns(n)].reshape(IJ, COLS)
 
-    def halves(count, tile, drive, over_den, t_, l_, one, two):
+    def halves(count, tile, drive, over_den, t_, b_, c_, two):
         @pl.loop(0, CHUNKS)
         def _(n):
             t1 = dot(tile[...], w_cols(n))
             t_[:, columns(n)] = t1.astype(BF16)
             b1 = (drive(n) + t1) * over_den[:, columns(n)]
             high = b1.astype(BF16)
-            l_[0:count, columns(n)] = high
-            l_[count : 2 * count, columns(n)] = (b1 - high.astype(F32)).astype(BF16)
+            b_[0:count, columns(n)] = high
+            b_[count : 2 * count, columns(n)] = (b1 - high.astype(F32)).astype(BF16)
 
         @pl.loop(0, CHUNKS)
         def _(n):
             turned = dot(t_[...], perm[:, columns(n)]) * over_den[:, columns(n)]
-            l_[2 * count : 3 * count, columns(n)] = turned.astype(BF16)
+            c_[:, columns(n)] = turned.astype(BF16)
 
         @pl.loop(0, CHUNKS)
         def _(n):
-            both = dot(l_[...], w_cols(n))
-            one[:, columns(n)] = both[0:count] + both[count : 2 * count]
-            two[:, columns(n)] = both[2 * count :].astype(BF16)
+            two[:, columns(n)] = dot(c_[...], w_cols(n)).astype(BF16)
+
+    def joined(n, count, b_, two):
+        both = dot(b_[...], w_cols(n))
+        return both[0:count] + both[count : 2 * count] + dot(two[...], perm[:, columns(n)])
 
     def drive(n):
         return drv[:, :, columns(n)].astype(F32).reshape(ROWS, COLS)
 
-    halves(ROWS, ab, drive, rden, tb, lhs, x1, x2b)
+    halves(ROWS, ab, drive, rden, tb, lhs, cb, x2b)
 
     for n in range(CHUNKS):
         cols = slice(n * COLS, (n + 1) * COLS)
-        zz = x1[:, cols] + dot(x2b[...], perm[:, cols])
+        zz = joined(n, ROWS, lhs, x2b)
         x1[:, cols] = drv[:, :, cols].astype(F32).reshape(ROWS, COLS) + zz
         zsend[n] = zz.reshape(2, 8, 8, COLS).astype(BF16)
         for h in range(2):
@@ -288,10 +292,9 @@
     def early_drive(n):
         return draw[:, :, :, columns(n)].astype(F32).reshape(EROWS, COLS)
 
-    halves(EROWS, ab2, early_drive, rden2, tb2, lhs2, x12, x2b2)
+    halves(EROWS, ab2, early_drive, rden2, tb2, lhs2, cb2, x2b2)
     for n in range(CHUNKS):
-        cols = slice(n * COLS, (n + 1) * COLS)
-        zz = x12[:, cols] + dot(x2b2[...], perm[:, cols])
+        zz = joined(n, EROWS, lhs2, x2b2)
         zrecv[n, :, 0:EARLY] = zz.reshape(2, EARLY, 8, COLS).astype(BF16)
 
     for n in range(CHUNKS):
@@ -332,7 +335,7 @@
     dma = pltpu.SemaphoreType.DMA
     return pl.pallas_call(
         kernel,
-        out_shape=jax.ShapeDtypeStruct(amplitudes.shape, F32),
+        out_shape=pltpu.VMEM(amplitudes.shape, F32),
         in_specs=[hbm, hbm, vmem, smem, smem, smem],
         out_specs=vmem,
         scratch_shapes=[
@@ -347,7 +350,8 @@
             pltpu.VMEM((ROWS, IJ), F32),
             pltpu.VMEM((ROWS, IJ), BF16),
             pltpu.VMEM((ROWS, IJ), BF16),
-            pltpu.VMEM((3 * ROWS, IJ), BF16),
+            pltpu.VMEM((2 * ROWS, IJ), BF16),
+            pltpu.VMEM((ROWS, IJ), BF16),
             pltpu.VMEM((ROWS, IJ), F32),
             pltpu.VMEM((ROWS, IJ), BF16),
             pltpu.VMEM((CHUNKS, 2, 8, 8, COLS), BF16),
@@ -358,8 +362,8 @@
             pltpu.VMEM((EROWS, IJ), F32),
             pltpu.VMEM((EROWS, IJ), BF16),
             pltpu.VMEM((EROWS, IJ), BF16),
-            pltpu.VMEM((3 * EROWS, IJ), BF16),
-            pltpu.VMEM((EROWS, IJ), F32),
+            pltpu.VMEM((2 * EROWS, IJ), BF16),
+            pltpu.VMEM((EROWS, IJ), BF16),
             pltpu.VMEM((EROWS, IJ), BF16),
             dma((2,)),
             dma((2, 2)),

time: 60.5 us -> 58.2 us (0.962)
  the two profiles are of different devices: /device:TPU:49 before, /device:TPU:81 now
where the time goes in v4:
time: 58.2 us; the launch traced here: 58 us
  Pallas kernels  57.2 us (98%)
  local copies, waits for them, and re-layouts  0.8 us (1%)
    pallas_call x1, Pallas kernels, on_device(): pl.pallas_call(kernel, out_shape=pltpu.VMEM(amplitudes.shape, F32), in_sp...  57.2 us

profile of v4, /device:TPU:81, one launch (start us, length us, event | category | flops | bytes accessed | tf_op | source)
XLA Modules:
  0.0 58.0 jit_solution(12377459958649926472)
XLA Ops:
  0.0 57.2 %shard_map.64 = f32[16,8,1024]{2,1,0:T(8,128)S(1)} custom-call(f32[16,8,1024]{2,1,0:T(8,128)} %amp_hbm.1, bf16[16,8,1024]{2,1,0:T(8,128)(2,1)} %drv_hbm.1, bf16[32,64]{1,0:T(8,128)(2,1)} %bitcast.1, s32[16,16]{1,0:T(8,128)} %mask.1, f32[256]{0:T(256)} %ve.1, f32[32]{0:T(128)} %oe.1), custom_call_target="tpu_custom_call" | custom-call | tf_op jit(solution)/shard_map/pallas_call | solution.py:336
  57.2 0.8 %copy.8 = f32[16,8,1024]{2,1,0:T(8,128)} copy(f32[16,8,1024]{2,1,0:T(8,128)S(1)} %shard_map.64) | data formatting | bytes 1048576

commit v5 on v4

--- a/solution.py
+++ b/solution.py
@@ -49,7 +49,8 @@
 
 
 def kernel(
-    amp_hbm, drv_hbm, lad, mask, ve, oe, out,
+    amp_hbm, drv_hbm, lad_hbm, mask_hbm, ve_hbm, oe_hbm, out,
+    lad, mask, ve, oe,
     G, W, perm, shuf, blk, amp, drv, abt, rden, ab, tb, lhs, cb, x1, x2b, zsend, zrecv, vs,
     araw, draw, rden2, ab2, tb2, lhs2, cb2, x2b2, in_s, r_ss, r_rs, z_ss, z_rs, f_ss, f_rs, s_ss, s_rs, c_ss, c_rs, e_ss, e_rs,
 ):
@@ -79,22 +80,24 @@
     for peer in peers:
         pl.semaphore_signal(barrier, inc=1, device_id=peer, device_id_type=MESH)
 
-    loads = [
-        pltpu.make_async_copy(amp_hbm, amp, in_s.at[0]),
-        pltpu.make_async_copy(drv_hbm, drv, in_s.at[1]),
-    ]
+    pairs = ((lad_hbm, lad), (mask_hbm, mask), (ve_hbm, ve), (oe_hbm, oe), (amp_hbm, amp), (drv_hbm, drv))
+    loads = [pltpu.make_async_copy(src, dst, in_s.at[i]) for i, (src, dst) in enumerate(pairs)]
     for load in loads:
         load.start()
 
+    eye = onehot(iota((64, 64), 0) == iota((64, 64), 1))
+    spread = onehot((iota((O, 128), 1) & (O - 1)) == iota((O, 128), 0))
+    group = iota((16, 128), 1) >> 5
+    for load in loads[:4]:
+        load.wait()
     keep = mask[p, lax.div(q, 2)].astype(F32)
-    eye = onehot(iota((64, 64), 0) == iota((64, 64), 1))
     rows = lax.dot_general(
         eye, lad[...], (((1,), (1,)), ((), ())), preferred_element_type=F32
     ).astype(BF16)
-    packed = jnp.zeros((16, 128), F32)
-    for t in range(4):
-        place = onehot(iota((32, 128), 1) == iota((32, 128), 0) + 32 * t)
-        packed = packed + dot(rows[16 * t : 16 * t + 16, :], place)
+    four = dot(rows, spread)
+    packed = four[0:16]
+    for t in range(1, 4):
+        packed = jnp.where(group == t, four[16 * t : 16 * t + 16], packed)
     packed = (packed * keep).astype(BF16)
     blk[...] = packed
     G[zh, zl, k, x, y] = packed
@@ -167,7 +170,7 @@
         r = iota((512, 512), 0)
         c = iota((512, 512), 1)
         shuf[...] = onehot(c == ((r >> 5) & 3) * 128 + (r >> 7) * 32 + (r & 31))
-        loads[0].wait()
+        loads[4].wait()
         ab[...] = amp[...].reshape(ROWS, IJ).astype(BF16)
         abt[...] = amp[...].astype(BF16)
 
@@ -200,7 +203,7 @@
             for a in range(EARLY):
                 r = 8 * (s * EARLY + a)
                 rden2[r : r + 8, :] = 1.0 / (base + ve[q * 8 + a])
-        loads[1].wait()
+        loads[5].wait()
 
     def give(src, dst, ss, rs, h):
         to = (lax.div(q, 2), 2 * p + h)
@@ -232,7 +235,7 @@
 
     steps = [first, second, third, use, early]
     for i, (kind, n) in enumerate(plan()):
-        if i == 1:
+        if i == 9:
             prepare()
         steps[kind](n)
 
@@ -330,15 +333,18 @@
 
 def on_device(amplitudes, driving, ladder, block_mask, virt_energy, occ_energy):
     vmem = pl.BlockSpec(memory_space=pltpu.VMEM)
-    smem = pl.BlockSpec(memory_space=pltpu.SMEM)
     hbm = pl.BlockSpec(memory_space=pltpu.HBM)
     dma = pltpu.SemaphoreType.DMA
     return pl.pallas_call(
         kernel,
         out_shape=pltpu.VMEM(amplitudes.shape, F32),
-        in_specs=[hbm, hbm, vmem, smem, smem, smem],
+        in_specs=[hbm] * 6,
         out_specs=vmem,
         scratch_shapes=[
+            pltpu.VMEM((O, 64), BF16),
+            pltpu.SMEM(block_mask.shape, jnp.int32),
+            pltpu.SMEM(virt_energy.shape, F32),
+            pltpu.SMEM(occ_energy.shape, F32),
             pltpu.VMEM((NH, NH, 2, NX, NX, 16, 128), BF16),
             pltpu.VMEM((16, 4, 16, IJ), BF16),
             pltpu.VMEM((IJ, IJ), BF16),
@@ -365,7 +371,7 @@
             pltpu.VMEM((2 * EROWS, IJ), BF16),
             pltpu.VMEM((EROWS, IJ), BF16),
             pltpu.VMEM((EROWS, IJ), BF16),
-            dma((2,)),
+            dma((6,)),
             dma((2, 2)),
             dma((2, 2)),
             dma((NZ,)),

time: 58.2 us -> 57.1 us (0.981)
  Pallas kernels: 57.2 us -> 56.1 us
    pallas_call x1, Pallas kernels: 57.2 us -> 56.1 us  [on_device(): pl.pallas_call(kernel, out_shape=pltpu.VMEM(amplitudes.shape, F32), in_sp...]
where the time goes in v5:
time: 57.1 us; the launch traced here: 56.9 us
  Pallas kernels  56.1 us (98%)
  local copies, waits for them, and re-layouts  0.8 us (1%)
    pallas_call x1, Pallas kernels, on_device(): pl.pallas_call(kernel, out_shape=pltpu.VMEM(amplitudes.shape, F32), in_sp...  56.1 us

profile of v5, /device:TPU:81, one launch (start us, length us, event | category | flops | bytes accessed | tf_op | source)
XLA Modules:
  0.0 56.9 jit_solution(5180444054707484910)
XLA Ops:
  0.0 56.1 %shard_map.64 = f32[16,8,1024]{2,1,0:T(8,128)S(1)} custom-call(f32[16,8,1024]{2,1,0:T(8,128)} %amp_hbm.1, bf16[16,8,1024]{2,1,0:T(8,128)(2,1)} %drv_hbm.1, bf16[32,64]{1,0:T(8,128)(2,1)} %bitcast.1, s32[16,16]{1,0:T(8,128)} %mask_hbm.1, f32[256]{0:T(256)} %ve_hbm.1, f32[32]{0:T(128)} %oe_hbm.1), custom_call_target="tpu_custom_call" | custom-call | tf_op jit(solution)/shard_map/pallas_call | solution.py:338
  56.1 0.8 %copy.8 = f32[16,8,1024]{2,1,0:T(8,128)} copy(f32[16,8,1024]{2,1,0:T(8,128)S(1)} %shard_map.64) | data formatting | bytes 1048576

commit v6 on v5

--- a/solution.py
+++ b/solution.py
@@ -248,8 +248,7 @@
         return W[:, :, :, columns(n)].reshape(IJ, COLS)
 
     def halves(count, tile, drive, over_den, t_, b_, c_, two):
-        @pl.loop(0, CHUNKS)
-        def _(n):
+        for n in range(CHUNKS):
             t1 = dot(tile[...], w_cols(n))
             t_[:, columns(n)] = t1.astype(BF16)
             b1 = (drive(n) + t1) * over_den[:, columns(n)]
@@ -257,13 +256,11 @@
             b_[0:count, columns(n)] = high
             b_[count : 2 * count, columns(n)] = (b1 - high.astype(F32)).astype(BF16)
 
-        @pl.loop(0, CHUNKS)
-        def _(n):
+        for n in range(CHUNKS):
             turned = dot(t_[...], perm[:, columns(n)]) * over_den[:, columns(n)]
             c_[:, columns(n)] = turned.astype(BF16)
 
-        @pl.loop(0, CHUNKS)
-        def _(n):
+        for n in range(CHUNKS):
             two[:, columns(n)] = dot(c_[...], w_cols(n)).astype(BF16)
 
     def joined(n, count, b_, two):
@@ -278,7 +275,6 @@
     for n in range(CHUNKS):
         cols = slice(n * COLS, (n + 1) * COLS)
         zz = joined(n, ROWS, lhs, x2b)
-        x1[:, cols] = drv[:, :, cols].astype(F32).reshape(ROWS, COLS) + zz
         zsend[n] = zz.reshape(2, 8, 8, COLS).astype(BF16)
         for h in range(2):
             given.append(
@@ -286,6 +282,7 @@
                     zsend.at[n, h, EARLY:8], zrecv.at[n, k, EARLY:8], e_ss.at[n, h], e_rs.at[n, k], h
                 )
             )
+        x1[:, cols] = drv[:, :, cols].astype(F32).reshape(ROWS, COLS) + zz
 
     for s in range(2):
         for j, dst in enumerate((araw, draw)):

time: 57.1 us -> 55.3 us (0.968)
  Pallas kernels: 56.1 us -> 54.4 us
    pallas_call x1, Pallas kernels: 56.1 us -> 54.4 us  [on_device(): pl.pallas_call(kernel, out_shape=pltpu.VMEM(amplitudes.shape, F32), in_sp...]
where the time goes in v6:
time: 55.3 us; the launch traced here: 55.2 us
  Pallas kernels  54.4 us (98%)
  local copies, waits for them, and re-layouts  0.8 us (1%)
    pallas_call x1, Pallas kernels, on_device(): pl.pallas_call(kernel, out_shape=pltpu.VMEM(amplitudes.shape, F32), in_sp...  54.4 us

profile of v6, /device:TPU:81, one launch (start us, length us, event | category | flops | bytes accessed | tf_op | source)
XLA Modules:
  0.0 55.2 jit_solution(7206905923829611564)
XLA Ops:
  0.0 54.4 %shard_map.64 = f32[16,8,1024]{2,1,0:T(8,128)S(1)} custom-call(f32[16,8,1024]{2,1,0:T(8,128)} %amp_hbm.1, bf16[16,8,1024]{2,1,0:T(8,128)(2,1)} %drv_hbm.1, bf16[32,64]{1,0:T(8,128)(2,1)} %bitcast.1, s32[16,16]{1,0:T(8,128)} %mask_hbm.1, f32[256]{0:T(256)} %ve_hbm.1, f32[32]{0:T(128)} %oe_hbm.1), custom_call_target="tpu_custom_call" | custom-call | tf_op jit(solution)/shard_map/pallas_call | solution.py:335
  54.4 0.8 %copy.8 = f32[16,8,1024]{2,1,0:T(8,128)} copy(f32[16,8,1024]{2,1,0:T(8,128)S(1)} %shard_map.64) | data formatting | bytes 1048576

commit v7 on v6

--- a/solution.py
+++ b/solution.py
@@ -148,23 +148,32 @@
         copy(piece, piece, c_ss, c_rs.at[n], sibling).start()
 
     def use(n):
-        h_, l_ = plane(GROUPS[n])
-        wait_bytes(G.at[0, 0, 0], c_rs.at[n])
+        if n % 2 == 0:
+            return
+        planes = [plane(GROUPS[m]) for m in (n - 1, n)]
+        for m in (n - 1, n):
+            wait_bytes(G.at[0, 0, 0], c_rs.at[m])
         wide = jnp.concatenate(
             [
                 jnp.concatenate(
                     [G[h_, l_, j % 2, :, 2 * g + j // 2].reshape(64, 128) for j in range(4)], axis=1
                 )
+                for h_, l_ in planes
                 for g in range(2)
             ],
             axis=0,
         )
         moved = dot(wide, shuf[...]).astype(BF16)
-        cols = pl.ds(pl.multiple_of(l_ * COLS, COLS), COLS)
-        for t in range(4):
-            W[pl.ds(h_ * NX, NX), t, :, cols] = jnp.concatenate(
-                [moved[64 * g : 64 * g + 64, 128 * t : 128 * t + 128] for g in range(2)], axis=1
-            ).reshape(NX, 16, COLS)
+        for i, (h_, l_) in enumerate(planes):
+            cols = pl.ds(pl.multiple_of(l_ * COLS, COLS), COLS)
+            for t in range(4):
+                W[pl.ds(h_ * NX, NX), t, :, cols] = jnp.concatenate(
+                    [
+                        moved[64 * (2 * i + g) : 64 * (2 * i + g) + 64, 128 * t : 128 * t + 128]
+                        for g in range(2)
+                    ],
+                    axis=1,
+                ).reshape(NX, 16, COLS)
 
     def prepare():
         r = iota((512, 512), 0)

time: 55.3 us -> 55.6 us (level)
  no operation moved by 1% of the time
where the time goes in v7:
time: 55.6 us; the launch traced here: 55.4 us
  Pallas kernels  54.6 us (98%)
  local copies, waits for them, and re-layouts  0.8 us (1%)
    pallas_call x1, Pallas kernels, on_device(): pl.pallas_call(kernel, out_shape=pltpu.VMEM(amplitudes.shape, F32), in_sp...  54.6 us

profile of v7, /device:TPU:81, one launch (start us, length us, event | category | flops | bytes accessed | tf_op | source)
XLA Modules:
  0.0 55.4 jit_solution(11549133561477849624)
XLA Ops:
  0.0 54.6 %shard_map.64 = f32[16,8,1024]{2,1,0:T(8,128)S(1)} custom-call(f32[16,8,1024]{2,1,0:T(8,128)} %amp_hbm.1, bf16[16,8,1024]{2,1,0:T(8,128)(2,1)} %drv_hbm.1, bf16[32,64]{1,0:T(8,128)(2,1)} %bitcast.1, s32[16,16]{1,0:T(8,128)} %mask_hbm.1, f32[256]{0:T(256)} %ve_hbm.1, f32[32]{0:T(128)} %oe_hbm.1), custom_call_target="tpu_custom_call" | custom-call | tf_op jit(solution)/shard_map/pallas_call | solution.py:344
  54.6 0.8 %copy.8 = f32[16,8,1024]{2,1,0:T(8,128)} copy(f32[16,8,1024]{2,1,0:T(8,128)S(1)} %shard_map.64) | data formatting | bytes 1048576
